TPU v7x, 32 devices: a whole 2x2x4 slice. The times are simulated.
32 devices in a mesh: grp: 2 (over x), dp: 8 (over z, y), tp: 2 (over core).
Axes of the slice: x: 2, y: 2, z: 4, core: 2. Of those that a mesh axis runs over, the one named last changes fastest.
Arguments:
- frames: bfloat16 [2, 16, 128, 1280], P('grp', ('dp', 'tp')), may hold values from -12 to 12
- counts: int32 [16], P('dp'), may hold values from 0 to 1, as said below
- w_qkv: bfloat16 [2, 1280, 3840], P('grp'), may hold values from -0.18727069 to 0.18727069
- ln_gain: bfloat16 [2, 1280], P('grp'), may hold values from 0.5 to 1.5
- w_proj: bfloat16 [2, 5120, 8192], P('grp', 'dp', 'tp'), may hold values from -1.5931984 to 1.5931984
- rms_gain: bfloat16 [2, 8192], P('grp', 'tp'), may hold values from 0.5 to 1.5
- cotangent: bfloat16 [2, 512, 8192], P('grp', 'dp', 'tp'), may hold values from -6 to 6
Outputs:
- frame_grad: bfloat16 [2, 16, 128, 1280], P('grp', ('dp', 'tp'))
Inputs may be any that keep to these rules, and one draw needn't show every extreme that they name: `counts`: some encoder device has all 1 frames live.
All inputs are finite; a program needn't handle non-finite values.
Results may differ from a plain program's by a relative error of at most 0.025.
Values may be sent and summed in bfloat16 or wider, within the bound.
No kernel may reach another device: no remote copies, remote signals or barrier semaphores. Data moves between devices by JAX's collectives and lax.ppermute only.
A program may use at most 128 MiB of HBM per device.

v0:
```python
import jax
import jax.numpy as jnp
from jax import lax
from jax.sharding import PartitionSpec as P

HEADS = 16
HDIM = 80
D = 8192


def passed_along(block, axis, distance):
    devices = range(lax.axis_size(axis))
    route = [(i - distance, i) for i in devices if i - distance in devices]
    return lax.ppermute(block, axis, route)


def encoder_forward(frames, w_qkv, ln_gain):
    frame_count = frames.shape[0]
    length = frames.shape[1]
    vis_width = frames.shape[2]
    mixed_qkv = jnp.einsum("fpe,ec->fpc", frames, w_qkv, preferred_element_type=jnp.float32).astype(
        jnp.bfloat16
    )
    split_heads = mixed_qkv.reshape(frame_count, length, 3, HEADS, HDIM)
    scores = jnp.einsum(
        "fqhd,fkhd->fhqk",
        split_heads[:, :, 0],
        split_heads[:, :, 1],
        preferred_element_type=jnp.float32,
    ) * HDIM ** (-0.5)
    attn_probs = jax.nn.softmax(scores, axis=-1)
    weights = attn_probs.astype(jnp.bfloat16)
    attended = jnp.einsum(
        "fhqk,fkhd->fqhd", weights, split_heads[:, :, 2], preferred_element_type=jnp.float32
    )
    summed = frames.astype(jnp.float32) + attended.reshape(frame_count, length, vis_width)
    centred = summed - jnp.mean(summed, axis=-1, keepdims=True)
    inverse = lax.rsqrt(jnp.mean(centred * centred, axis=-1, keepdims=True) + 1e-06)
    normal_part = centred * inverse
    embedded = (normal_part * ln_gain.astype(jnp.float32)).astype(jnp.bfloat16)
    return (
        embedded.reshape(frame_count * length // 4, 4 * vis_width),
        mixed_qkv,
        attn_probs,
        normal_part,
        inverse,
    )


def encoder_backward(w_qkv, ln_gain, mixed_qkv, attn_probs, normal_part, inverse, grad_embed):
    frame_count = normal_part.shape[0]
    length = normal_part.shape[1]
    vis_width = normal_part.shape[2]
    split_heads = mixed_qkv.reshape(frame_count, length, 3, HEADS, HDIM)
    query_heads = split_heads[:, :, 0]
    key_heads = split_heads[:, :, 1]
    value_heads = split_heads[:, :, 2]
    weights = attn_probs.astype(jnp.bfloat16)
    grad_norm = grad_embed.reshape(frame_count, length, vis_width).astype(
        jnp.float32
    ) * ln_gain.astype(jnp.float32)
    grad_summed = inverse * (
        grad_norm
        - jnp.mean(grad_norm, axis=-1, keepdims=True)
        - normal_part * jnp.mean(grad_norm * normal_part, axis=-1, keepdims=True)
    )
    grad_heads = grad_summed.astype(jnp.bfloat16).reshape(frame_count, length, HEADS, HDIM)
    grad_weights = jnp.einsum(
        "fqhd,fkhd->fhqk", grad_heads, value_heads, preferred_element_type=jnp.float32
    )
    grad_values = jnp.einsum(
        "fhqk,fqhd->fkhd", weights, grad_heads, preferred_element_type=jnp.float32
    ).astype(jnp.bfloat16)
    grad_scores = (
        attn_probs
        * (grad_weights - jnp.sum(grad_weights * attn_probs, axis=-1, keepdims=True))
        * HDIM ** (-0.5)
    ).astype(jnp.bfloat16)
    grad_query = jnp.einsum(
        "fhqk,fkhd->fqhd", grad_scores, key_heads, preferred_element_type=jnp.float32
    ).astype(jnp.bfloat16)
    grad_keys = jnp.einsum(
        "fhqk,fqhd->fkhd", grad_scores, query_heads, preferred_element_type=jnp.float32
    ).astype(jnp.bfloat16)
    grad_mixed = jnp.stack([grad_query, grad_keys, grad_values], axis=2).reshape(
        frame_count, length, 3 * vis_width
    )
    through = jnp.einsum("fpc,ec->fpe", grad_mixed, w_qkv, preferred_element_type=jnp.float32)
    return (grad_summed + through).astype(jnp.bfloat16)


def per_device(frames, counts, w_qkv, ln_gain, w_proj, rms_gain, cotangent):
    is_encoder = lax.axis_index("grp") == 0
    local_frames = frames[0]
    weight_mix = w_qkv[0]
    gain_ln = ln_gain[0]
    frame_count = local_frames.shape[0]
    length = local_frames.shape[1]
    vis_width = local_frames.shape[2]
    merged_width = 4 * vis_width
    tokens_frame = length // 4
    tokens_here = frame_count * tokens_frame

    def run_encoder():
        return encoder_forward(local_frames, weight_mix, gain_ln)

    def skip_encoder():
        return (
            jnp.zeros((tokens_here, merged_width), jnp.bfloat16),
            jnp.zeros((frame_count, length, 3 * vis_width), jnp.bfloat16),
            jnp.zeros((frame_count, HEADS, length, length), jnp.float32),
            jnp.zeros((frame_count, length, vis_width), jnp.float32),
            jnp.zeros((frame_count, length, 1), jnp.float32),
        )

    embedded, mixed_qkv, attn_probs, normal_part, inverse = lax.cond(
        is_encoder, run_encoder, skip_encoder
    )
    arrived = passed_along(embedded, "grp", 1)
    pooled = lax.all_gather(arrived, "tp", axis=0, tiled=True)
    full_proj = lax.all_gather(w_proj[0], "dp", axis=0, tiled=True)
    row_count = pooled.shape[0]
    col_count = full_proj.shape[1]
    activations = lax.cond(
        is_encoder,
        lambda: jnp.zeros((row_count, col_count), jnp.float32),
        lambda: jnp.dot(pooled, full_proj, preferred_element_type=jnp.float32),
    )
    tp_count = lax.axis_size("tp")
    position = lax.broadcasted_iota(jnp.int32, (row_count,), 0)
    source = position // tokens_here
    slot_index = position // tokens_frame % frame_count
    owner_hits = source[:, None] == lax.broadcasted_iota(jnp.int32, (1, tp_count), 1)
    live_limit = jnp.sum(jnp.where(owner_hits, counts[None, :], 0), axis=1)
    live_mask = (slot_index < live_limit).astype(jnp.float32)
    scaled = (
        rms_gain[0].astype(jnp.float32)[None, :]
        * cotangent[0].astype(jnp.float32)
        * live_mask[:, None]
    )
    squares = jnp.sum(activations * activations, axis=1)
    products = jnp.sum(activations * scaled, axis=1)
    total_sq, total_prod = lax.psum((squares, products), "tp")
    inverse_rms = lax.rsqrt(total_sq / D + 1e-06)[:, None]
    product = (total_prod / D)[:, None]
    grad_acts = (inverse_rms * scaled - activations * inverse_rms**3 * product).astype(jnp.bfloat16)
    term_rows = lax.cond(
        is_encoder,
        lambda: jnp.zeros((row_count, merged_width), jnp.bfloat16),
        lambda: lax.dot_general(
            grad_acts, full_proj, (((1,), (1,)), ((), ())), preferred_element_type=jnp.float32
        ).astype(jnp.bfloat16),
    )
    rounded_terms = lax.optimization_barrier(term_rows)
    summed_rows = lax.psum_scatter(
        rounded_terms.astype(jnp.float32).astype(jnp.bfloat16),
        "tp",
        scatter_dimension=0,
        tiled=True,
    )
    returned = passed_along(summed_rows, "grp", -1)
    grad_frames = lax.cond(
        is_encoder,
        lambda: encoder_backward(
            weight_mix, gain_ln, mixed_qkv, attn_probs, normal_part, inverse, returned
        ),
        lambda: jnp.zeros(local_frames.shape, jnp.bfloat16),
    )
    return grad_frames[None]


def solution(mesh):
    placed = (
        P("grp", ("dp", "tp"), None, None),
        P("dp"),
        P("grp", None, None),
        P("grp", None),
        P("grp", "dp", "tp"),
        P("grp", "tp"),
        P("grp", "dp", "tp"),
    )
    return jax.shard_map(
        per_device,
        mesh=mesh,
        in_specs=placed,
        out_specs=P("grp", ("dp", "tp"), None, None),
        check_vma=False,
    )
```

profile of v0, /device:TPU:0, one launch (start us, length us, event | category | flops | bytes accessed | tf_op | source)
XLA Modules:
  0.0 887.2 jit_solution(567608343134886291)
XLA Ops:
  6.5 0.7 all-gather.3.cloned.1.call-update
  7.3 0.7 reduce.10
  8.0 19.9 %conditional.4 = (bf16[32,5120]{1,0:T(8,128)(2,1)}, bf16[1,128,3840]{2,1,0:T(8,128)(2,1)}, f32[1,16,128,128]{2,3,1,0:T(8,128)S(1)}, f32[1,128,1280]{2,1,0:T(8,128)S(1)}, f32[1,128,1]{1,2,0:T(1,128)S(1)}) conditional(s32[]{:T(128)} %convert_element_type.147, () %tuple.34, (bf16[1,1,128,1280]{3,2,1,0:T(8,128)(2,1)}, bf16[1280,3840]{1,0:T(8,128)(2,1)}, ...), branch_computations={%region_0.0_spmd, %region_1.0_spmd} | conditional | flops 1389332864 | bytes 39174724 | solution.py:116
  8.1 6.4 convolution_convert_fusion
  14.5 1.6 copy.33
  16.1 1.5 fusion.32
  17.6 1.4 convolution_multiply_fusion
  18.9 0.2 copy.36
  19.1 2.2 add_reduce_fusion
  21.3 0.2 copy.37
  21.5 0.2 multiply_reduce_fusion
  21.8 0.1 broadcast_multiply_fusion
  21.9 0.1 mul.117
  22.0 0.2 mul.118
  22.2 0.1 sub.62
  22.3 1.0 sub.63
  23.4 0.5 copy.35
  23.9 0.6 reshape.363
  24.5 0.2 reshape.373
  24.7 1.9 multiply_convert_fusion
  26.6 1.3 fusion.6
  28.0 1.3 collective-permute-start
  29.3 0.1 fusion.31
  29.4 8.0 collective-permute-done
  37.4 2.3 all_gather.6
  39.7 767.0 %all-gather.3.cloned.1.call-done = bf16[1,5120,4096]{2,1,0:T(8,128)(2,1)} async-done(((bf16[1,640,4096]{2,1,0:T(8,128)(2,1)}), bf16[1,5120,4096]{2,1,0:T(8,128)(2,1)}) %all-gather.3.cloned.1.call-update) | async-done | bytes 41943056 | tf_op jit(solution)/shard_map/all_gather | solution.py:121
  806.7 0.1 conditional.5
  806.7 1.4 multiply_reduce_fusion.3
  808.1 2.5 all-reduce
  810.6 1.4 fusion.29
  812.0 0.2 conditional.6
  812.2 0.8 copy-done.2
  813.1 43.7 %reduce-scatter.2.cloned.1.call-done = bf16[32,5120]{1,0:T(8,128)(2,1)} async-done(((bf16[64,5120]{1,0:T(8,128)(2,1)}), bf16[32,5120]{1,0:T(8,128)(2,1)}) %reduce-scatter.2.cloned.1.call-update) | async-done | bytes 327696 | tf_op jit(solution)/shard_map/reduce_scatter | solution.py:155
  856.8 1.3 collective-permute-start.1
  858.1 10.6 %collective-permute-done.1 = bf16[32,5120]{1,0:T(8,128)(2,1)S(1)} collective-permute-done((bf16[32,5120]{1,0:T(8,128)(2,1)}, bf16[32,5120]{1,0:T(8,128)(2,1)S(1)}, u32[]{:S(2)}, u32[]{:S(2)}) %collective-permute-start.1) | collective-permute-done | bytes 327712 | tf_op jit(solution)/shard_map/ppermute | solution.py:14
  868.6 11.7 %conditional.7 = (bf16[1,1,128,1280]{3,2,1,0:T(8,128)(2,1)}) conditional(s32[]{:T(128)} %convert_element_type.147, () %tuple.33, (f32[1,128,1]{1,2,0:T(1,128)S(1)}, bf16[32,5120]{1,0:T(8,128)(2,1)S(1)}, bf16[1280]{0:T(1024)(128)(2,1)S(1)}, f32[1,128,1280]{2,1,0:T(8,128)S(1)}, bf16[1,128,3840]{2,1,0:T(8,128)(2,1)}, ...), branch_computations={%region_16.17_spmd, %region_17.21_spmd} | conditional | flops 1432157440 | bytes 69775912 | solution.py:162
  868.6 0.2 reshape.376
  868.8 0.2 multiply_reduce_fusion.2
  869.0 0.2 fusion.24
  869.2 0.9 copy.38
  870.1 1.6 copy.42
  871.7 1.5 fusion.19
  873.2 0.2 fusion.20
  873.4 0.3 fusion.16
  873.8 0.5 fusion.14
  874.3 1.8 fusion.15
  876.1 0.1 pad_maximum_fusion
  876.2 4.1 fusion.13
  (24 shorter events, 0.3 us)
Async XLA Ops:
  6.5 800.1 %all-gather.3.cloned.1.call-start = ((), (), s32[]{:S(2)}) async-start(), calls=%async_computation.2 | async-start | bytes 47185920 | tf_op jit(solution)/shard_map/all_gather | solution.py:121
  7.3 849.5 %reduce-scatter.2.cloned.1.call-start = ((), (), s32[]{:S(2)}) async-start(), calls=%async_computation.1 | async-start | bytes 983040 | tf_op jit(solution)/shard_map/reduce_scatter | solution.py:155
  8.0 21.2 %copy-start.3 = (bf16[1,4096]{1,0:T(2,128)(2,1)S(1)}, bf16[1,4096]{1,0:T(2,128)(2,1)}, u32[]{:S(2)}) copy-start(bf16[1,4096]{1,0:T(2,128)(2,1)} %param.20) | copy-start | bytes 24580
  8.0 21.3 %copy-start.4 = (s32[2]{0:T(128)S(1)}, s32[2]{0:T(128)}, u32[]{:S(2)}) copy-start(s32[2]{0:T(128)} %param.16) | copy-start | bytes 28
  8.1 10.9 %copy-start.1 = (bf16[1,1,128,1280]{3,2,1,0:T(8,128)(2,1)S(1)}, bf16[1,1,128,1280]{3,2,1,0:T(8,128)(2,1)}, u32[]{:S(2)}) copy-start(bf16[1,1,128,1280]{3,2,1,0:T(8,128)(2,1)} %get-tuple-element.69) | copy-start | bytes 983044 | tf_op jit(solution)/shard_map/cond
  28.0 9.5 %collective-permute-start = (bf16[32,5120]{1,0:T(8,128)(2,1)}, bf16[32,5120]{1,0:T(8,128)(2,1)S(1)}, u32[]{:S(2)}, u32[]{:S(2)}) collective-permute-start(bf16[32,5120]{1,0:T(8,128)(2,1)} %get-tuple-element.64), channel_id=1, source_target_pairs={{0,16},{1,17},{2,18},{3,19},{4,20},{5,21},{6,22},{7,23},{8,24},{9,... | collective-permute-start | bytes 983048 | tf_op jit(solution)/shard_map/ppermute | solution.py:14
  812.2 0.8 copy-start.2
  856.8 11.9 %collective-permute-start.1 = (bf16[32,5120]{1,0:T(8,128)(2,1)}, bf16[32,5120]{1,0:T(8,128)(2,1)S(1)}, u32[]{:S(2)}, u32[]{:S(2)}) collective-permute-start(bf16[32,5120]{1,0:T(8,128)(2,1)} %reduce-scatter.2.cloned.1.call-done), channel_id=1, source_target_pairs={{16,0},{17,1},{18,2},{19,3},{20,4},{21,5},{22,6},{23,7},{24,8},{25... | collective-permute-start | bytes 983048 | tf_op jit(solution)/shard_map/ppermute | solution.py:14
  871.7 4.5 copy-start
Sparse Core Ops, SparseCore 0:
  8.9 797.7 all-gather.2
  813.2 43.5 reduce-scatter.1
where the time goes:
time: 888 us; the launch traced here: 887 us
  waiting for transfers between devices  830 us (93%)
  matrix products  19.7 us (2%)
  between operations  13.5 us (2%)
    all_gather x1, waiting for transfers between devices, per_device(): full_proj = lax.all_gather(w_proj[0], 'dp', axis=0, tiled=True)  767 us
    reduce_scatter x1, waiting for transfers between devices, per_device(): lax.psum_scatter(rounded_terms.astype(jnp.float32).astype(jnp.bfloat16),...  43.7 us
    ppermute x2, waiting for transfers between devices, passed_along(): return lax.ppermute(block, axis, route)  18.6 us
  transfers between devices with their start and end apart: 4, of which 4 were waited for; matrix products, arithmetic and copies ran while one was open for 2% of the time, Pallas kernels for 0%

commit v1 on v0

--- a/solution.py
+++ b/solution.py
@@ -118,7 +118,15 @@
     )
     arrived = passed_along(embedded, "grp", 1)
     pooled = lax.all_gather(arrived, "tp", axis=0, tiled=True)
-    full_proj = lax.all_gather(w_proj[0], "dp", axis=0, tiled=True)
+    ways, here = (lax.axis_size("dp"), lax.axis_index("dp"))
+    grown, reach = (w_proj[0], 1)
+    while reach < ways:
+        theirs = lax.ppermute(grown, "dp", [(d, d ^ reach) for d in range(ways)])
+        mine_first = jnp.concatenate([grown, theirs], axis=0)
+        theirs_first = jnp.concatenate([theirs, grown], axis=0)
+        grown = jnp.where(here & reach == 0, mine_first, theirs_first)
+        reach = 2 * reach
+    full_proj = grown
     row_count = pooled.shape[0]
     col_count = full_proj.shape[1]
     activations = lax.cond(

time: 888 us -> 1420 us (1.60)
  waiting for transfers between devices: 830 us -> 1270 us
  other arithmetic: 7.89 us -> 87.9 us
    ppermute x0 -> x3, waiting for transfers between devices: none -> 1210 us  [per_device(): theirs = lax.ppermute(grown, 'dp', [(d, d ^ reach) for d in range(ways)])]
    all_gather x1 -> x0, waiting for transfers between devices: 767 us -> none  [per_device(): full_proj = lax.all_gather(w_proj[0], 'dp', axis=0, tiled=True)]
    select_n x0 -> x3, other arithmetic: none -> 80.5 us  [per_device(): grown = jnp.where(here & reach == 0, mine_first, theirs_first)]
  transfers between devices with their start and end apart: 4 -> 6, of which waited for: 4 -> 6; matrix products, arithmetic and copies ran while one was open for 2% -> 1% of each run, Pallas kernels for 0% -> 0%
where the time goes in v1:
time: 1420 us
  waiting for transfers between devices  1270 us (89%)
  other arithmetic  87.9 us (6%)
  matrix products  22.6 us (2%)
    ppermute x3, waiting for transfers between devices, per_device(): theirs = lax.ppermute(grown, 'dp', [(d, d ^ reach) for d in range(ways)])  1210 us
    select_n x3, other arithmetic, per_device(): grown = jnp.where(here & reach == 0, mine_first, theirs_first)  80.5 us
    reduce_scatter x1, waiting for transfers between devices, per_device(): lax.psum_scatter(rounded_terms.astype(jnp.float32).astype(jnp.bfloat16),...  44.5 us
  transfers between devices with their start and end apart: 6, of which 6 were waited for; matrix products, arithmetic and copies ran while one was open for 1% of the time, Pallas kernels for 0%

profile of v1, /device:TPU:0, one launch (start us, length us, event | category | flops | bytes accessed | tf_op | source)
XLA Modules:
  0.0 1415.8 jit_solution(12103879833148762540)
XLA Ops:
  6.5 3.0 collective-permute-start.1
  9.5 113.4 %collective-permute-done.1 = bf16[640,4096]{1,0:T(8,128)(2,1)} collective-permute-done((bf16[640,4096]{1,0:T(8,128)(2,1)}, bf16[640,4096]{1,0:T(8,128)(2,1)}, u32[]{:S(2)}, u32[]{:S(2)}) %collective-permute-start.1) | collective-permute-done | bytes 5242912 | tf_op jit(solution)/shard_map/ppermute | solution.py:124
  122.9 13.7 maximum_select_fusion.2
  136.5 1.8 collective-permute-start.2
  138.3 225.1 %collective-permute-done.2 = bf16[1280,4096]{1,0:T(8,128)(2,1)} collective-permute-done((bf16[1280,4096]{1,0:T(8,128)(2,1)}, bf16[1280,4096]{1,0:T(8,128)(2,1)}, u32[]{:S(2)}, u32[]{:S(2)}) %collective-permute-start.2) | collective-permute-done | bytes 10485792 | tf_op jit(solution)/shard_map/ppermute | solution.py:124
  363.4 21.8 %maximum_select_fusion.1 = bf16[2560,4096]{1,0:T(8,128)(2,1)} fusion(bf16[1280,4096]{1,0:T(8,128)(2,1)} %collective-permute-done.2, bf16[1280,4096]{1,0:T(8,128)(2,1)} %maximum_select_fusion.2, pred[]{:T(512)S(6)} %eq.29), kind=kLoop, calls=%fused_computation.55 | loop fusion | flops 94371840 | bytes 41943040 | tf_op jit(solution)/shard_map/jit(_where)/select_n | solution.py:127
  385.2 2.6 collective-permute-start.3
  387.9 20.7 %conditional.4 = (bf16[32,5120]{1,0:T(8,128)(2,1)}, bf16[1,128,3840]{2,1,0:T(8,128)(2,1)}, f32[1,16,128,128]{2,3,1,0:T(8,128)S(1)}, f32[1,128,1280]{2,1,0:T(8,128)S(1)}, f32[1,128,1]{1,2,0:T(1,128)S(1)}) conditional(s32[]{:T(128)} %convert_element_type.147, () %tuple.34, (bf16[1,1,128,1280]{3,2,1,0:T(8,128)(2,1)S(1)}, bf16[1280,3840]{1,0:T(8,128)(2,1)}, ...), branch_computations={%region_0.0_spmd, %region_1.0_spmd} | conditional | flops 1389332864 | bytes 37863976 | solution.py:116
  387.9 6.2 convolution_convert_fusion
  394.1 1.6 copy.33
  395.7 1.5 fusion.32
  397.2 1.4 convolution_multiply_fusion
  398.6 0.2 copy.36
  398.7 2.1 add_reduce_fusion
  400.8 0.2 copy.37
  401.1 0.2 multiply_reduce_fusion
  401.6 1.0 mul.118
  402.7 1.0 sub.63
  403.7 0.5 copy.35
  404.2 0.6 reshape.363
  404.8 0.2 reshape.373
  405.1 2.1 multiply_convert_fusion
  407.2 1.3 fusion.6
  408.5 1.3 collective-permute-start
  410.0 5.3 collective-permute-done
  415.3 2.3 all_gather.3
  417.6 868.7 %collective-permute-done.3 = bf16[2560,4096]{1,0:T(8,128)(2,1)} collective-permute-done((bf16[2560,4096]{1,0:T(8,128)(2,1)}, bf16[2560,4096]{1,0:T(8,128)(2,1)}, u32[]{:S(2)}, u32[]{:S(2)}) %collective-permute-start.3) | collective-permute-done | bytes 20971552 | tf_op jit(solution)/shard_map/ppermute | solution.py:124
  1286.3 45.1 %maximum_select_fusion = bf16[5120,4096]{1,0:T(8,128)(2,1)} fusion(bf16[2560,4096]{1,0:T(8,128)(2,1)} %collective-permute-done.3, bf16[2560,4096]{1,0:T(8,128)(2,1)} %maximum_select_fusion.1, pred[]{:T(512)S(6)} %eq.28), kind=kLoop, calls=%fused_computation.54 | loop fusion | flops 188743680 | bytes 83886080 | tf_op jit(solution)/shard_map/jit(_where)/select_n | solution.py:127
  1331.4 0.3 conditional.5
  1331.6 1.4 multiply_reduce_fusion.3
  1333.0 2.5 all-reduce
  1335.5 1.4 fusion.29
  1337.0 0.8 copy-done.1
  1337.8 44.5 %reduce-scatter.2.cloned.1.call-done = bf16[32,5120]{1,0:T(8,128)(2,1)} async-done(((bf16[64,5120]{1,0:T(8,128)(2,1)}), bf16[32,5120]{1,0:T(8,128)(2,1)}) %reduce-scatter.2.cloned.1.call-update) | async-done | bytes 327696 | tf_op jit(solution)/shard_map/reduce_scatter | solution.py:163
  1382.3 1.3 collective-permute-start.4
  1383.5 10.6 collective-permute-done.4
  1394.1 14.8 %conditional.7 = (bf16[1,1,128,1280]{3,2,1,0:T(8,128)(2,1)}) conditional(s32[]{:T(128)} %convert_element_type.147, () %tuple.33, (f32[1,128,1]{1,2,0:T(1,128)S(1)}, bf16[32,5120]{1,0:T(8,128)(2,1)S(1)}, bf16[1280]{0:T(1024)(128)(2,1)S(1)}, f32[1,128,1280]{2,1,0:T(8,128)S(1)}, bf16[1,128,3840]{2,1,0:T(8,128)(2,1)}, ...), branch_computations={%region_16.17_spmd, %region_17.21_spmd} | conditional | flops 1432157440 | bytes 30454280 | solution.py:170
  1394.1 0.2 reshape.376
  1394.3 0.2 multiply_reduce_fusion.2
  1394.5 0.2 fusion.24
  1394.7 0.9 copy.38
  1395.6 1.6 copy.42
  1397.2 1.3 fusion.19
  1398.5 0.2 fusion.20
  1398.8 0.3 fusion.16
  1399.1 0.5 fusion.14
  1399.6 1.5 fusion.15
  1401.2 7.8 fusion.13
  (30 shorter events, 0.9 us)
Async XLA Ops:
  6.5 1375.7 %reduce-scatter.2.cloned.1.call-start = ((), (), s32[]{:S(2)}) async-start(), calls=%async_computation.1 | async-start | bytes 983040 | tf_op jit(solution)/shard_map/reduce_scatter | solution.py:163
  6.5 116.3 %collective-permute-start.1 = (bf16[640,4096]{1,0:T(8,128)(2,1)}, bf16[640,4096]{1,0:T(8,128)(2,1)}, u32[]{:S(2)}, u32[]{:S(2)}) collective-permute-start(bf16[640,4096]{1,0:T(8,128)(2,1)} %bitcast.136), channel_id=1, source_target_pairs={{0,2},{2,0},{4,6},{6,4},{8,10},{10,8},{12,14},{14,12},{1,3},{3,1},... | collective-permute-start | bytes 15728648 | tf_op jit(solution)/shard_map/ppermute | solution.py:124
  136.5 226.9 %collective-permute-start.2 = (bf16[1280,4096]{1,0:T(8,128)(2,1)}, bf16[1280,4096]{1,0:T(8,128)(2,1)}, u32[]{:S(2)}, u32[]{:S(2)}) collective-permute-start(bf16[1280,4096]{1,0:T(8,128)(2,1)} %maximum_select_fusion.2), channel_id=1, source_target_pairs={{0,4},{2,6},{4,0},{6,2},{8,12},{10,14},{12,8},{14,10},{1,5},{3,7},... | collective-permute-start | bytes 31457288 | tf_op jit(solution)/shard_map/ppermute | solution.py:124
  138.3 249.5 %copy-start.3 = (bf16[1,1280]{1,0:T(2,128)(2,1)S(1)}, bf16[1,1280]{1,0:T(2,128)(2,1)}, u32[]{:S(2)}) copy-start(bf16[1,1280]{1,0:T(2,128)(2,1)} %param.18) | copy-start | bytes 7684
  138.3 249.5 %copy-start = (bf16[1,1,128,1280]{3,2,1,0:T(8,128)(2,1)S(1)}, bf16[1,1,128,1280]{3,2,1,0:T(8,128)(2,1)}, u32[]{:S(2)}) copy-start(bf16[1,1,128,1280]{3,2,1,0:T(8,128)(2,1)} %param.15) | copy-start | bytes 983044
  385.2 901.1 %collective-permute-start.3 = (bf16[2560,4096]{1,0:T(8,128)(2,1)}, bf16[2560,4096]{1,0:T(8,128)(2,1)}, u32[]{:S(2)}, u32[]{:S(2)}) collective-permute-start(bf16[2560,4096]{1,0:T(8,128)(2,1)} %maximum_select_fusion.1), channel_id=1, source_target_pairs={{0,8},{2,10},{4,12},{6,14},{8,0},{10,2},{12,4},{14,6},{1,9},{3,11}... | collective-permute-start | bytes 62914568 | tf_op jit(solution)/shard_map/ppermute | solution.py:124
  387.8 22.0 %copy-start.2 = (bf16[1,4096]{1,0:T(2,128)(2,1)S(1)}, bf16[1,4096]{1,0:T(2,128)(2,1)}, u32[]{:S(2)}) copy-start(bf16[1,4096]{1,0:T(2,128)(2,1)} %param.20) | copy-start | bytes 24580
  387.8 22.1 %copy-start.4 = (s32[2]{0:T(128)S(1)}, s32[2]{0:T(128)}, u32[]{:S(2)}) copy-start(s32[2]{0:T(128)} %param.16) | copy-start | bytes 28
  408.5 6.8 collective-permute-start
  1336.9 0.8 copy-start.1
  1382.3 11.9 collective-permute-start.4
Sparse Core Ops, SparseCore 0:
  1337.9 44.2 reduce-scatter.1
